TPU v7x, 512 devices: a whole 4x8x8 slice. The times are simulated.
512 devices in a mesh: dp: 2 (over y_lo), row: 8 (over y_hi, core), col: 32 (over z, x).
Axes of the slice: x: 4, y: 8 (y_hi: 4, y_lo: 2; y = y_hi * 2 + y_lo), z: 8, core: 2. Of those that a mesh axis runs over, the one named last changes fastest.
Arguments:
- gate_pre: bfloat16 [2048, 28672], P(('dp', 'row'), 'col'), may hold values from -6 to 6
- up_pre: bfloat16 [2048, 28672], P(('dp', 'row'), 'col'), may hold values from -6 to 6
- grad_out: bfloat16 [2048, 16384], P('col', ('dp', 'row')), may hold values from -6 to 6
- down_weight: bfloat16 [28672, 16384], P('col', ('dp', 'row')), may hold values from -0.046875 to 0.046875
- basis: bfloat16 [512, 28672], P(('dp', 'row'), 'col'), may hold values from -0.0625 to 0.0625
- first_moment_in: float32 [512, 16384], P('col', ('dp', 'row')), may hold values from -6 to 6
- second_moment_in: float32 [512, 16384], P('col', ('dp', 'row')), may hold values from 0.1 to 10
Outputs:
- grad_gate: bfloat16 [2048, 28672], P(('dp', 'row'), 'col')
- grad_up: bfloat16 [2048, 28672], P(('dp', 'row'), 'col')
- scaled_grad: bfloat16 [28672, 16384], P('col', ('dp', 'row'))
- first_moment: float32 [512, 16384], P('col', ('dp', 'row'))
- second_moment: float32 [512, 16384], P('col', ('dp', 'row'))
All inputs are finite; a program needn't handle non-finite values.
Results may differ from a plain program's by a relative error of at most 0.024.
Values may be sent and summed in bfloat16 or wider, within the bound.
No kernel may reach another device: no remote copies, remote signals or barrier semaphores. Data moves between devices by JAX's collectives and lax.ppermute only.
A program may use at most 64 MiB of HBM per device.

v0:
```python
import math

import jax
import jax.numpy as jnp
from jax import lax
from jax.sharding import PartitionSpec as P

first_fix = 1.0 - math.exp(1000.0 * math.log(0.9))
second_fix = 1.0 - math.exp(1000.0 * math.log(0.999))


def adam_rows(first_in, second_in, projected):
    first_new = 0.9 * first_in + 0.1 * projected
    second_new = 0.999 * second_in + 0.001 * projected * projected
    adapted = first_new / first_fix / (jnp.sqrt(second_new / second_fix) + 1e-06)
    return (first_new, second_new, adapted)


def shards(gate_pre, up_pre, grad_out, down_weight, basis, first_moment_in, second_moment_in):
    gate_f = gate_pre.astype(jnp.float32)
    up_f = up_pre.astype(jnp.float32)
    sigma = jax.nn.sigmoid(gate_f)
    act_value = gate_f * sigma
    hidden = (act_value * up_f).astype(jnp.bfloat16)
    cotangent = lax.all_gather(grad_out, "col", axis=0, tiled=True)
    out_rows = cotangent
    summed = lax.psum_scatter(
        lax.dot_general(
            out_rows, down_weight, (((1,), (1,)), ((), ())), preferred_element_type=jnp.float32
        ).astype(jnp.bfloat16),
        ("dp", "row"),
        scatter_dimension=0,
        tiled=True,
    )
    grad_hidden = summed.astype(jnp.float32)
    grad_up = (grad_hidden * act_value).astype(jnp.bfloat16)
    grad_gate = (grad_hidden * up_f * sigma * (1.0 + gate_f * (1.0 - sigma))).astype(jnp.bfloat16)
    out_rows = cotangent
    weight_exact = lax.dot_general(
        lax.all_gather(hidden, ("dp", "row"), axis=0, tiled=True),
        out_rows,
        (((0,), (0,)), ((), ())),
        preferred_element_type=jnp.float32,
    )
    grad_weight = weight_exact.astype(jnp.bfloat16)
    basis_full = lax.all_gather(basis, ("dp", "row"), axis=0, tiled=True)
    own_rows = first_moment_in.shape[0]
    partial_proj = jnp.dot(
        basis_full.astype(jnp.float32), weight_exact, precision=lax.Precision.HIGHEST
    )
    projected_all = lax.psum(partial_proj.astype(jnp.bfloat16), "col").astype(jnp.float32)
    row_offset = lax.axis_index("col") * own_rows
    projected = lax.dynamic_slice_in_dim(projected_all, row_offset, own_rows, 0)
    first_moment, second_moment, adapted = adam_rows(first_moment_in, second_moment_in, projected)
    adapted_sq, projected_sq = lax.psum(
        (jnp.sum(adapted * adapted, axis=0), jnp.sum(projected * projected, axis=0)), "col"
    )
    column_scale = jnp.sqrt(adapted_sq) / (jnp.sqrt(projected_sq) + 1e-06)
    scaled_grad = (grad_weight.astype(jnp.float32) * column_scale[None, :]).astype(jnp.bfloat16)
    return (grad_gate, grad_up, scaled_grad, first_moment, second_moment)


def solution(mesh):
    placed = (
        P(("dp", "row"), "col"),
        P(("dp", "row"), "col"),
        P("col", ("dp", "row")),
        P("col", ("dp", "row")),
        P(("dp", "row"), "col"),
        P("col", ("dp", "row")),
        P("col", ("dp", "row")),
    )
    return jax.shard_map(
        shards,
        mesh=mesh,
        in_specs=placed,
        out_specs=(
            P(("dp", "row"), "col"),
            P(("dp", "row"), "col"),
            P("col", ("dp", "row")),
            P("col", ("dp", "row")),
            P("col", ("dp", "row")),
        ),
        check_vma=False,
    )
```

profile of v0, /device:TPU:8, one launch (start us, length us, event | category | flops | bytes accessed | tf_op | source)
XLA Modules:
  0.0 534.4 jit_solution(7834187348341108367)
XLA Ops:
  7.2 0.0 copy-start
  7.2 0.0 all-gather.3.cloned.1.call-start
  7.2 0.7 all-gather.3.cloned.1.call-update
  7.9 0.0 reduce-scatter.2.cloned.1.call-start
  8.0 95.8 %all-gather.3.cloned.1.call-done = bf16[2048,1024]{1,0:T(8,128)(2,1)} async-done(((bf16[64,1024]{1,0:T(8,128)(2,1)}), bf16[2048,1024]{1,0:T(8,128)(2,1)}) %all-gather.3.cloned.1.call-update) | async-done | bytes 4194320 | tf_op jit(solution)/shard_map/all_gather | solution.py:25
  103.8 8.3 %convolution_convert_fusion = bf16[2048,896]{1,0:T(8,128)(2,1)} fusion(bf16[2048,1024]{1,0:T(8,128)(2,1)} %all-gather.3.cloned.1.call-done, bf16[896,1024]{1,0:T(8,128)(2,1)S(1)} %copy-done), kind=kOutput, calls=%fused_computation.1 | convolution fusion | flops 3759931392 | bytes 9699328 | tf_op jit(solution)/shard_map/dot_general | solution.py:28
  112.1 0.0 reduce-scatter.2.cloned.1.call-update
  112.1 0.0 all-gather.5.cloned.1.call-start
  112.1 78.2 %reduce-scatter.2.cloned.1.call-done = bf16[128,896]{1,0:T(8,128)(2,1)} async-done(((bf16[2048,896]{1,0:T(8,128)(2,1)}), bf16[128,896]{1,0:T(8,128)(2,1)}) %reduce-scatter.2.cloned.1.call-update) | async-done | bytes 229392 | tf_op jit(solution)/shard_map/reduce_scatter | solution.py:27
  190.3 0.0 copy-done.2
  190.3 2.0 fusion.5
  192.4 0.0 all-gather.5.cloned.1.call-update
  192.4 0.0 all-reduce.3.cloned.1.call-start
  192.5 23.8 %all_gather.11 = bf16[512,896]{1,0:T(8,128)(2,1)S(1)} all-gather(bf16[32,896]{1,0:T(8,128)(2,1)S(1)} %copy-done.6), channel_id=1, replica_groups=mesh['dp'=2,'row'=8,'col'=32] {'dp','row'}, dimensions={0}, use_global_device_ids=true | all-gather | bytes 974848 | tf_op jit(solution)/shard_map/all_gather | solution.py:46
  216.3 56.0 %all-gather.5.cloned.1.call-done = bf16[2048,896]{1,0:T(8,128)(2,1)} async-done(((bf16[128,896]{1,0:T(8,128)(2,1)}), bf16[2048,896]{1,0:T(8,128)(2,1)}) %all-gather.5.cloned.1.call-update) | async-done | bytes 3670032 | tf_op jit(solution)/shard_map/all_gather | solution.py:40
  272.3 6.9 %fusion.15 = f32[896,1024]{1,0:T(8,128)S(1)} fusion(bf16[2048,896]{1,0:T(8,128)(2,1)} %all-gather.5.cloned.1.call-done, bf16[2048,1024]{1,0:T(8,128)(2,1)} %all-gather.3.cloned.1.call-done), kind=kOutput, calls=%fused_computation.28 | convolution fusion | flops 3758096384 | bytes 11534336 | tf_op jit(solution)/shard_map/dot_general | solution.py:39
  279.2 1.8 copy-done.1
  281.0 4.5 fusion
  285.5 0.0 all-reduce.3.cloned.1.call-update
  285.5 163.8 %all-reduce.3.cloned.1.call-done = bf16[512,1024]{1,0:T(8,128)(2,1)} async-done(((bf16[512,1024]{1,0:T(8,128)(2,1)}), bf16[512,1024]{1,0:T(8,128)(2,1)}) %all-reduce.3.cloned.1.call-update) | async-done | bytes 1048592 | tf_op jit(solution)/shard_map/psum | solution.py:51
  449.3 0.0 copy-done.5
  449.3 1.5 multiply_reduce_fusion
  450.7 73.3 %all-reduce = (f32[1024]{0:T(1024)S(1)}, f32[1024]{0:T(1024)S(1)}) all-reduce(f32[1024]{0:T(1024)S(1)} %get-tuple-element.15, f32[1024]{0:T(1024)S(1)} %get-tuple-element.12), channel_id=1, replica_groups=mesh['dp'=2,'row'=8,'col'=32] {'col'}, use_global_device_ids=true, to_apply=%region_5.0 | all-reduce | flops 2048 | bytes 16384 | tf_op jit(solution)/shard_map/psum | solution.py:55
  524.1 3.8 multiply_convert_fusion
  (11 shorter events, 0.0 us)
Async XLA Ops:
  7.2 96.6 %copy-start = (bf16[896,1024]{1,0:T(8,128)(2,1)S(1)}, bf16[896,1024]{1,0:T(8,128)(2,1)}, u32[]{:S(2)}) copy-start(bf16[896,1024]{1,0:T(8,128)(2,1)} %param.10) | copy-start | bytes 5505028
  7.2 96.6 %all-gather.3.cloned.1.call-start = ((), (), s32[]{:S(2)}) async-start(), calls=%async_computation.1 | async-start | bytes 4325376 | tf_op jit(solution)/shard_map/all_gather | solution.py:25
  7.9 182.4 %reduce-scatter.2.cloned.1.call-start = ((), (), s32[]{:S(2)}) async-start(), calls=%async_computation.2 | async-start | bytes 3899392 | tf_op jit(solution)/shard_map/reduce_scatter | solution.py:27
  112.0 78.3 %copy-start.2 = (bf16[128,896]{1,0:T(8,128)(2,1)S(1)}, bf16[128,896]{1,0:T(8,128)(2,1)}, u32[]{:S(2)}) copy-start(bf16[128,896]{1,0:T(8,128)(2,1)} %param.8) | copy-start | bytes 688132
  112.0 78.3 %copy-start.3 = (bf16[128,896]{1,0:T(8,128)(2,1)S(1)}, bf16[128,896]{1,0:T(8,128)(2,1)}, u32[]{:S(2)}) copy-start(bf16[128,896]{1,0:T(8,128)(2,1)} %param.7) | copy-start | bytes 688132
  112.0 80.4 %copy-start.6 = (bf16[32,896]{1,0:T(8,128)(2,1)S(1)}, bf16[32,896]{1,0:T(8,128)(2,1)}, u32[]{:S(2)}) copy-start(bf16[32,896]{1,0:T(8,128)(2,1)} %param.11) | copy-start | bytes 172036
  112.1 160.2 %all-gather.5.cloned.1.call-start = ((), (), s32[]{:S(2)}) async-start(), calls=%async_computation.3 | async-start | bytes 3899392 | tf_op jit(solution)/shard_map/all_gather | solution.py:40
  192.4 256.9 %all-reduce.3.cloned.1.call-start = ((), (), s32[]{:S(2)}) async-start(), calls=%async_computation.4 | async-start | bytes 2097152 | tf_op jit(solution)/shard_map/psum | solution.py:51
  279.2 1.8 copy-start.1
  281.0 168.3 %copy-start.4 = (f32[16,1024]{1,0:T(8,128)S(1)}, f32[16,1024]{1,0:T(8,128)}, u32[]{:S(2)}) copy-start(f32[16,1024]{1,0:T(8,128)} %param.13) | copy-start | bytes 196612
  281.0 168.3 %copy-start.5 = (f32[16,1024]{1,0:T(8,128)S(1)}, f32[16,1024]{1,0:T(8,128)}, u32[]{:S(2)}) copy-start(f32[16,1024]{1,0:T(8,128)} %param.12) | copy-start | bytes 196612
Sparse Core Ops, SparseCore 0:
  11.2 92.5 all-gather.2
  112.2 78.0 reduce-scatter.1
  193.0 79.2 all-gather.4
  285.6 163.5 all-reduce.2
where the time goes:
time: 535 us; the launch traced here: 534 us
  waiting for transfers between devices  395 us (74%)
  blocking collectives  97.1 us (18%)
  matrix products  19.7 us (4%)
  between operations  13.8 us (3%)
  other arithmetic  7.26 us (1%)
    psum x1, waiting for transfers between devices, shards(): lax.psum(partial_proj.astype(jnp.bfloat16), 'col').astype(jnp.float32)  164 us
    all_gather x1, waiting for transfers between devices, shards(): cotangent = lax.all_gather(grad_out, 'col', axis=0, tiled=True)  95.8 us
    reduce_scatter x1, waiting for transfers between devices, shards(): lax.psum_scatter(lax.dot_general(out_rows, down_weight, (((1,), (1,)), ((...  78.2 us
    psum x1, blocking collectives, shards(): lax.psum((jnp.sum(adapted * adapted, axis=0), jnp.sum(projected * project...  73.3 us
    all_gather x1, waiting for transfers between devices, shards(): lax.all_gather(hidden, ('dp', 'row'), axis=0, tiled=True)  56 us
    all_gather x1, blocking collectives, shards(): basis_full = lax.all_gather(basis, ('dp', 'row'), axis=0, tiled=True)  23.8 us
  transfers between devices with their start and end apart: 4, of which 4 were waited for; matrix products, arithmetic and copies ran while one was open for 0% of the time, Pallas kernels for 0%

commit v1 on v0

v1 whole, which is shorter than its diff:
```python
import math

import jax
import jax.numpy as jnp
from jax import lax
from jax.experimental import pallas as pl
from jax.experimental.pallas import tpu as pltpu
from jax.sharding import PartitionSpec as P


first_fix = 1.0 - math.exp(1000.0 * math.log(0.9))
second_fix = 1.0 - math.exp(1000.0 * math.log(0.999))

BF = jnp.bfloat16
F32 = jnp.float32
TOK = ("dp", "row")
Z_GROUPS = [[4 * z + x for z in range(8)] for x in range(4)]
Y_GROUPS = [[2 * m + q for m in range(8)] for q in range(2)]
PAIR = [(k, k ^ 1) for k in range(16)]
CHUNKS = ((0, 24), (24, 64))


def along_x(value, step):
    return lax.ppermute(value, "col", [(c, c - c % 4 + (c % 4 + step) % 4) for c in range(32)])


def activation(gate_pre, up_pre):
    gate_f = gate_pre.astype(F32)
    sigma = jax.nn.sigmoid(gate_f)
    return gate_f, sigma, gate_f * sigma, up_pre.astype(F32)


def dot_nt(left, right):
    return lax.dot_general(left, right, (((1,), (1,)), ((), ())), preferred_element_type=F32)


def dot_tn(left, right):
    return lax.dot_general(left, right, (((0,), (0,)), ((), ())), preferred_element_type=F32)


def place_kernel(x_ref, here, left, right, far_low, far_high, out, sems):
    x = x_ref[0]
    half = far_low.shape[0]
    copies = []
    for piece, back, rows in (
        (here, 0, None),
        (left, 1, None),
        (right, 3, None),
        (far_low, 2, pl.ds(0, half)),
        (far_high, 2, pl.ds(half, half)),
    ):
        source = lax.rem(x + 4 - back, 4)
        target = out.at[:, source] if rows is None else out.at[rows, source]
        copies.append(pltpu.make_async_copy(piece, target, sems.at[len(copies)]))
    for copy in copies:
        copy.start()
    for copy in copies:
        copy.wait()


def place(x, pieces):
    planes, rows, width = pieces[0].shape
    return pl.pallas_call(
        place_kernel,
        out_shape=jax.ShapeDtypeStruct((planes, 4, rows, width), pieces[0].dtype),
        in_specs=[pl.BlockSpec(memory_space=pltpu.SMEM)] + [pl.BlockSpec(memory_space=pl.ANY)] * 5,
        out_specs=pl.BlockSpec(memory_space=pl.ANY),
        scratch_shapes=[pltpu.SemaphoreType.DMA((5,))],
        name="place",
    )(x[None], *pieces)


def gather_rows(value, x):
    sent = jnp.broadcast_to(value[None], (8,) + value.shape).reshape((-1,) + value.shape[1:])
    here = lax.all_to_all(sent, "col", 0, 0, tiled=True, axis_index_groups=Z_GROUPS)
    here = here.reshape((8,) + value.shape)
    left = along_x(here, 1)
    right = along_x(here, -1)
    far_low = along_x(left[:4], 1)
    far_high = along_x(right[4:], -1)
    return place(x, (here, left, right, far_low, far_high))


def exact(left, right):
    high = left.astype(BF)
    rest = left - high.astype(F32)
    mid = rest.astype(BF)
    low = (rest - mid.astype(F32)).astype(BF)
    terms = lax.dot_general(
        jnp.concatenate([high, mid, low], axis=0), right, (((1,), (0,)), ((), ())), preferred_element_type=F32
    ).reshape(3, 16, right.shape[1])
    return terms[0] + (terms[1] + terms[2])


def work(gate_pre, up_pre, grad_out, down_weight, basis, first_moment_in, second_moment_in):
    width = grad_out.shape[1]
    units = gate_pre.shape[1]
    core = lax.axis_index("row") % 2
    x = lax.axis_index("col") % 4

    _, _, act_early, up_early = activation(gate_pre, up_pre)
    hidden = (act_early * up_early).astype(BF)
    hidden_all = lax.all_gather(hidden, TOK, axis=0, tiled=True).reshape(32, 64, units)
    basis_all = lax.all_gather(basis, TOK, axis=0, tiled=True)
    tp_part = dot_nt(basis_all, hidden).astype(BF)
    tp_got = lax.all_to_all(tp_part, "col", 0, 0, tiled=True).reshape(32, 16, 128)
    tp_mine = jnp.sum(tp_got.astype(F32), axis=0)
    tp_all = lax.all_gather(tp_mine, TOK, axis=1, tiled=True).reshape(16, 32, 64)

    out_rows, blocks = [], []
    for begin, end in CHUNKS:
        rows = end - begin
        out = gather_rows(grad_out[begin:end], x)
        out_rows.append(out.reshape(32 * rows, width))
        part = dot_nt(out_rows[-1], down_weight).astype(BF).reshape(8, 2, 2 * rows, units)
        part_mine = lax.dynamic_index_in_dim(part, core, 1, keepdims=False).reshape(16 * rows, units)
        part_other = lax.dynamic_index_in_dim(part, 1 - core, 1, keepdims=False).reshape(16 * rows, units)
        part_got = lax.ppermute(part_other, TOK, PAIR)
        part_sum = (part_mine.astype(F32) + part_got.astype(F32)).astype(BF)
        got = lax.all_to_all(part_sum, TOK, 0, 0, tiled=True, axis_index_groups=Y_GROUPS)
        blocks.append(jnp.sum(got.reshape(8, 2, rows, units).astype(F32), axis=0).astype(BF))
    summed = jnp.concatenate(blocks, axis=1).reshape(128, units)
    gate_late, up_late, summed = lax.optimization_barrier((gate_pre, up_pre, summed))
    gate_f, sigma, act_value, up_f = activation(gate_late, up_late)
    grad_hidden = summed.astype(F32)
    grad_up = (grad_hidden * act_value).astype(BF)
    grad_gate = (grad_hidden * up_f * sigma * (1.0 + gate_f * (1.0 - sigma))).astype(BF)

    projected = sum(
        exact(tp_all[:, :, begin:end].reshape(16, -1), rows) for (begin, end), rows in zip(CHUNKS, out_rows)
    )
    first_moment = 0.9 * first_moment_in + 0.1 * projected
    second_moment = 0.999 * second_moment_in + 0.001 * projected * projected
    adapted = first_moment / first_fix / (jnp.sqrt(second_moment / second_fix) + 1e-06)
    totals = jnp.stack([jnp.sum(adapted * adapted, axis=0), jnp.sum(projected * projected, axis=0)])
    for bit in (1, 2, 4, 8, 16):
        totals = totals + lax.ppermute(totals, "col", [(c, c ^ bit) for c in range(32)])
    column_scale = jnp.sqrt(totals[0]) / (jnp.sqrt(totals[1]) + 1e-06)

    terms = [dot_tn(hidden_all[:, begin:end].reshape(-1, units), out_rows[i]) for i, (begin, end) in enumerate(CHUNKS)]
    grad_weight = sum(terms).astype(BF)
    scaled_grad = (grad_weight.astype(F32) * column_scale[None, :]).astype(BF)
    return (grad_gate, grad_up, scaled_grad, first_moment, second_moment)


def solution(mesh):
    rows = P(TOK, "col")
    cols = P("col", TOK)
    return jax.shard_map(
        work,
        mesh=mesh,
        in_specs=(rows, rows, cols, cols, rows, cols, cols),
        out_specs=(rows, rows, cols, cols, cols),
        check_vma=False,
    )
```

time: 535 us -> 382 us (0.71)
  waiting for transfers between devices: 395 us -> 44.3 us
  Pallas kernels: 0 us -> 129 us
  starting transfers between devices: 0.16 us -> 79.6 us
  blocking collectives: 97.1 us -> 64.7 us
  local copies, waits for them, and re-layouts: 1.8 us -> 18.4 us
  other arithmetic: 7.26 us -> 13.3 us
    psum x1 -> x0, waiting for transfers between devices: 164 us -> none  [shards(): lax.psum(partial_proj.astype(jnp.bfloat16), 'col').astype(jnp.float32)]
    all_gather x2 -> x1, waiting for transfers between devices: 152 us -> 0.01 us  [work(): lax.all_gather(hidden, TOK, axis=0, tiled=True).reshape(32, 64, units)]
    pallas_call x0 -> x2, Pallas kernels: none -> 129 us  [place(): pl.pallas_call(place_kernel, out_shape=jax.ShapeDtypeStruct((planes, 4, r...]
    reduce_scatter x1 -> x0, waiting for transfers between devices: 78.2 us -> none  [shards(): lax.psum_scatter(lax.dot_general(out_rows, down_weight, (((1,), (1,)), ((...]
    psum x1 -> x0, blocking collectives: 73.3 us -> none  [shards(): lax.psum((jnp.sum(adapted * adapted, axis=0), jnp.sum(projected * project...]
    ppermute x0 -> x15, starting transfers between devices: none -> 48.7 us  [the longest x8 25.9 us: along_x(): lax.ppermute(value, 'col', [(c, c - c % 4 + (c % 4 + step) % 4) for c in...]
    all_gather x1 -> x2, blocking collectives: 23.8 us -> 64.7 us  [the longest x1 32.8 us: work(): lax.all_gather(tp_mine, TOK, axis=1, tiled=True).reshape(16, 32, 64)]
    all_to_all x0 -> x5, starting transfers between devices: none -> 30.8 us  [the longest x2 13.9 us: gather_rows(): lax.all_to_all(sent, 'col', 0, 0, tiled=True, axis_index_groups=Z_GROUPS)]
  transfers between devices with their start and end apart: 4 -> 21, of which waited for: 4 -> 8; matrix products, arithmetic and copies ran while one was open for 0% -> 9% of each run, Pallas kernels for 0% -> 34%
where the time goes in v1:
time: 382 us; the launch traced here: 381 us
  Pallas kernels  129 us (34%)
  starting transfers between devices  79.6 us (21%)
  blocking collectives  64.7 us (17%)
  waiting for transfers between devices  44.3 us (12%)
  local copies, waits for them, and re-layouts  18.4 us (5%)
  matrix products  16.6 us (4%)
  between operations  14.6 us (4%)
  other arithmetic  13.3 us (3%)
    pallas_call x2, Pallas kernels, place(): pl.pallas_call(place_kernel, out_shape=jax.ShapeDtypeStruct((planes, 4, r...  129 us
    all_gather x1, blocking collectives, work(): lax.all_gather(tp_mine, TOK, axis=1, tiled=True).reshape(16, 32, 64)  32.8 us
    all_gather x1, blocking collectives, work(): basis_all = lax.all_gather(basis, TOK, axis=0, tiled=True)  32 us
    ppermute x8, starting transfers between devices, along_x(): lax.ppermute(value, 'col', [(c, c - c % 4 + (c % 4 + step) % 4) for c in...  25.9 us
    all_to_all x2, waiting for transfers between devices, gather_rows(): lax.all_to_all(sent, 'col', 0, 0, tiled=True, axis_index_groups=Z_GROUPS)  25.9 us
    ppermute x5, starting transfers between devices, work(): lax.ppermute(totals, 'col', [(c, c ^ bit) for c in range(32)])  19 us
    ppermute x5, waiting for transfers between devices, work(): lax.ppermute(totals, 'col', [(c, c ^ bit) for c in range(32)])  15 us
    all_to_all x2, starting transfers between devices, gather_rows(): lax.all_to_all(sent, 'col', 0, 0, tiled=True, axis_index_groups=Z_GROUPS)  13.9 us
  transfers between devices with their start and end apart: 21, of which 8 were waited for; matrix products, arithmetic and copies ran while one was open for 9% of the time, Pallas kernels for 34%

profile of v1, /device:TPU:8, one launch (start us, length us, event | category | flops | bytes accessed | tf_op | source)
XLA Modules:
  0.0 380.9 jit_solution(4119953251705644610)
XLA Ops:
  8.9 10.3 %all-to-all-start = ((bf16[8,24,1024]{2,1,0:T(8,128)(2,1)}), bf16[8,24,1024]{2,1,0:T(8,128)(2,1)S(1)}, u32[]{:S(2)}, u32[]{:S(2)}) async-start(bf16[8,24,1024]{2,1,0:T(8,128)(2,1)} %broadcast_in_dim.7), calls=%async_computation | async-start | bytes 786432 | tf_op jit(solution)/shard_map/all_to_all | solution.py:75
  20.2 13.8 %all-to-all-done.here = bf16[8,24,1024]{2,1,0:T(8,128)(2,1)S(1)} async-done(((bf16[8,24,1024]{2,1,0:T(8,128)(2,1)}), bf16[8,24,1024]{2,1,0:T(8,128)(2,1)S(1)}, u32[]{:S(2)}, u32[]{:S(2)}) %all-to-all-start) | async-done | bytes 393248 | tf_op jit(solution)/shard_map/all_to_all | solution.py:75
  34.9 3.5 all-to-all-start.2
  39.4 4.8 %collective-permute-start.1 = (bf16[8,24,1024]{2,1,0:T(8,128)(2,1)S(1)}, bf16[8,24,1024]{2,1,0:T(8,128)(2,1)S(1)}, u32[]{:S(2)}, u32[]{:S(2)}) collective-permute-start(bf16[8,24,1024]{2,1,0:T(8,128)(2,1)S(1)} %all-to-all-done.here), channel_id=1, source_target_pairs={{0,3},{1,0},{2,1},{3,2},{4,7},{5,4},{6,5},{7,6},{8,11},{9,8},{10,9... | collective-permute-start | bytes 1179656 | tf_op jit(solution)/shard_map/ppermute | solution.py:24
  46.1 12.1 %all-to-all-done.2.here = bf16[8,40,1024]{2,1,0:T(8,128)(2,1)S(1)} async-done(((bf16[8,40,1024]{2,1,0:T(8,128)(2,1)}), bf16[8,40,1024]{2,1,0:T(8,128)(2,1)S(1)}, u32[]{:S(2)}, u32[]{:S(2)}) %all-to-all-start.2) | async-done | bytes 655392 | tf_op jit(solution)/shard_map/all_to_all | solution.py:75
  58.3 4.7 %collective-permute-start.6 = (bf16[8,40,1024]{2,1,0:T(8,128)(2,1)S(1)}, bf16[8,40,1024]{2,1,0:T(8,128)(2,1)}, u32[]{:S(2)}, u32[]{:S(2)}) collective-permute-start(bf16[8,40,1024]{2,1,0:T(8,128)(2,1)S(1)} %all-to-all-done.2.here), channel_id=1, source_target_pairs={{0,3},{1,0},{2,1},{3,2},{4,7},{5,4},{6,5},{7,6},{8,11},{9,8},{10,9... | collective-permute-start | bytes 1966088 | tf_op jit(solution)/shard_map/ppermute | solution.py:24
  64.9 32.0 %all_gather.10 = bf16[512,896]{1,0:T(8,128)(2,1)S(1)} all-gather(bf16[32,896]{1,0:T(8,128)(2,1)} %param.11), channel_id=1, replica_groups=mesh['dp'=2,'row'=8,'col'=32] {'dp','row'}, dimensions={0}, use_global_device_ids=true | all-gather | bytes 974848 | tf_op jit(solution)/shard_map/all_gather | solution.py:104
  102.0 3.1 collective-permute-start.2
  106.3 8.2 %all-to-all-start.4 = ((bf16[32,16,128]{2,1,0:T(8,128)(2,1)}), bf16[32,16,128]{2,1,0:T(8,128)(2,1)S(1)}, u32[]{:S(2)}, u32[]{:S(2)}) async-start(bf16[32,16,128]{2,1,0:T(8,128)(2,1)} %bitcast.18), calls=%async_computation.4 | async-start | bytes 262144 | tf_op jit(solution)/shard_map/all_to_all | solution.py:106
  114.6 48.8 %place.2 = bf16[8,4,24,1024]{3,2,1,0:T(8,128)(2,1)} custom-call(s32[1]{0:T(128)} %bitcast.x_ref, bf16[8,24,1024]{2,1,0:T(8,128)(2,1)} %copy-done.7, bf16[8,24,1024]{2,1,0:T(8,128)(2,1)} %collective-permute-done.left, bf16[8,24,1024]{2,1,0:T(8,128)(2,1)} %copy-done.10, bf16[4,24,1024]{2,1,0:T(8,128)(2,1)} %collective-permute-done.2.far_low, ...), custom_call_target="tpu_custom_call" | custom-call | tf_op jit(solution)/shard_map/place/pallas_call | solution.py:63
  164.4 4.9 %collective-permute-start.8 = (bf16[4,40,1024]{2,1,0:T(8,128)(2,1)S(1)}, bf16[4,40,1024]{2,1,0:T(8,128)(2,1)S(1)}, u32[]{:S(2)}, u32[]{:S(2)}) collective-permute-start(bf16[4,40,1024]{2,1,0:T(8,128)(2,1)S(1)} %slice.81), channel_id=1, source_target_pairs={{0,3},{1,0},{2,1},{3,2},{4,7},{5,4},{6,5},{7,6},{8,11},{9,8},{10,9... | collective-permute-start | bytes 983048 | tf_op jit(solution)/shard_map/ppermute | solution.py:24
  172.2 3.2 convolution_convert_fusion.1
  178.6 3.4 collective-permute-done.7.far_low
  182.7 80.6 %place.3 = bf16[8,4,40,1024]{3,2,1,0:T(8,128)(2,1)} custom-call(s32[1]{0:T(128)} %bitcast.x_ref, bf16[8,40,1024]{2,1,0:T(8,128)(2,1)} %copy-done.4, bf16[8,40,1024]{2,1,0:T(8,128)(2,1)} %collective-permute-done.5.left, bf16[8,40,1024]{2,1,0:T(8,128)(2,1)} %collective-permute-done.6.right, bf16[4,40,1024]{2,1,0:T(8,128)(2,1)} %copy-done.13, ...), custom_call_target="tpu_custom_call" | custom-call | tf_op jit(solution)/shard_map/place/pallas_call | solution.py:63
  263.3 4.7 %convolution_convert_fusion = bf16[1280,896]{1,0:T(8,128)(2,1)S(1)} fusion(bf16[1280,1024]{1,0:T(8,128)(2,1)} %bitcast.40, bf16[896,1024]{1,0:T(8,128)(2,1)S(1)} %copy-done), kind=kOutput, calls=%fused_computation.2 | convolution fusion | flops 2349957120 | bytes 6750208 | tf_op jit(solution)/shard_map/dot_general | solution.py:34
  273.3 4.2 %all-to-all-start.1 = ((bf16[8,48,896]{2,1,0:T(8,128)(2,1)}), bf16[8,48,896]{2,1,0:T(8,128)(2,1)}, u32[]{:S(2)}, u32[]{:S(2)}) async-start(bf16[8,48,896]{2,1,0:T(8,128)(2,1)} %bitcast.49), calls=%async_computation.1 | async-start | bytes 1376256 | tf_op jit(solution)/shard_map/all_to_all | solution.py:120
  277.5 32.8 %all_gather.11 = f32[16,2048]{1,0:T(8,128)S(1)} all-gather(f32[16,128]{1,0:T(8,128)S(1)} %convert_reduce_fusion), channel_id=1, replica_groups=mesh['dp'=2,'row'=8,'col'=32] {'dp','row'}, dimensions={1}, use_global_device_ids=true | all-gather | bytes 139264 | tf_op jit(solution)/shard_map/all_gather | solution.py:108
  313.9 4.6 %all-to-all-start.3 = ((bf16[8,80,896]{2,1,0:T(8,128)(2,1)}), bf16[8,80,896]{2,1,0:T(8,128)(2,1)}, u32[]{:S(2)}, u32[]{:S(2)}) async-start(bf16[8,80,896]{2,1,0:T(8,128)(2,1)} %bitcast.46), calls=%async_computation.3 | async-start | bytes 2293760 | tf_op jit(solution)/shard_map/all_to_all | solution.py:120
  326.1 3.6 collective-permute-done.10
  331.7 5.1 %collective-permute-done.11 = f32[2,1024]{1,0:T(2,128)S(1)} collective-permute-done((f32[2,1024]{1,0:T(2,128)S(1)}, f32[2,1024]{1,0:T(2,128)S(1)}, u32[]{:S(2)}, u32[]{:S(2)}) %collective-permute-start.11) | collective-permute-done | bytes 8224 | tf_op jit(solution)/shard_map/ppermute | solution.py:137
  336.8 3.4 collective-permute-start.12
  342.4 4.3 %collective-permute-start.13 = (f32[2,1024]{1,0:T(2,128)S(1)}, f32[2,1024]{1,0:T(2,128)S(1)}, u32[]{:S(2)}, u32[]{:S(2)}) collective-permute-start(f32[2,1024]{1,0:T(2,128)S(1)} %add.106), channel_id=1, source_target_pairs={{0,8},{1,9},{2,10},{3,11},{4,12},{5,13},{6,14},{7,15},{8,0},{9,1},... | collective-permute-start | bytes 24584 | tf_op jit(solution)/shard_map/ppermute | solution.py:137
  348.8 7.5 %collective-permute-start.14 = (f32[2,1024]{1,0:T(2,128)S(1)}, f32[2,1024]{1,0:T(2,128)S(1)}, u32[]{:S(2)}, u32[]{:S(2)}) collective-permute-start(f32[2,1024]{1,0:T(2,128)S(1)} %add.107), channel_id=1, source_target_pairs={{0,16},{1,17},{2,18},{3,19},{4,20},{5,21},{6,22},{7,23},{8,24},{9,... | collective-permute-start | bytes 24584 | tf_op jit(solution)/shard_map/ppermute | solution.py:137
  371.0 3.0 multiply_convert_fusion
  (102 shorter events, 60.0 us)
Async XLA Ops:
  7.2 165.1 %copy-start = (bf16[896,1024]{1,0:T(8,128)(2,1)S(1)}, bf16[896,1024]{1,0:T(8,128)(2,1)}, u32[]{:S(2)}) copy-start(bf16[896,1024]{1,0:T(8,128)(2,1)} %param.10) | copy-start | bytes 5505028
  8.9 25.0 %all-to-all-start = ((bf16[8,24,1024]{2,1,0:T(8,128)(2,1)}), bf16[8,24,1024]{2,1,0:T(8,128)(2,1)S(1)}, u32[]{:S(2)}, u32[]{:S(2)}) async-start(bf16[8,24,1024]{2,1,0:T(8,128)(2,1)} %broadcast_in_dim.7), calls=%async_computation | async-start | bytes 786432 | tf_op jit(solution)/shard_map/all_to_all | solution.py:75
  34.9 23.3 %all-to-all-start.2 = ((bf16[8,40,1024]{2,1,0:T(8,128)(2,1)}), bf16[8,40,1024]{2,1,0:T(8,128)(2,1)S(1)}, u32[]{:S(2)}, u32[]{:S(2)}) async-start(bf16[8,40,1024]{2,1,0:T(8,128)(2,1)} %broadcast_in_dim.8), calls=%async_computation.2 | async-start | bytes 1310720 | tf_op jit(solution)/shard_map/all_to_all | solution.py:75
  38.5 326.1 %all-gather.2.cloned.1.call-start = ((), (), s32[]{:S(2)}) async-start(), calls=%async_computation.5 | async-start | bytes 3899392 | tf_op jit(solution)/shard_map/all_gather | solution.py:103
  39.4 65.7 %copy-start.6 = (bf16[128,896]{1,0:T(8,128)(2,1)S(1)}, bf16[128,896]{1,0:T(8,128)(2,1)}, u32[]{:S(2)}) copy-start(bf16[128,896]{1,0:T(8,128)(2,1)} %fusion.15) | copy-start | bytes 688132
  39.4 57.4 %collective-permute-start.1 = (bf16[8,24,1024]{2,1,0:T(8,128)(2,1)S(1)}, bf16[8,24,1024]{2,1,0:T(8,128)(2,1)S(1)}, u32[]{:S(2)}, u32[]{:S(2)}) collective-permute-start(bf16[8,24,1024]{2,1,0:T(8,128)(2,1)S(1)} %all-to-all-done.here), channel_id=1, source_target_pairs={{0,3},{1,0},{2,1},{3,2},{4,7},{5,4},{6,5},{7,6},{8,11},{9,8},{10,9... | collective-permute-start | bytes 1179656 | tf_op jit(solution)/shard_map/ppermute | solution.py:24
  44.2 56.2 %collective-permute-start = (bf16[8,24,1024]{2,1,0:T(8,128)(2,1)S(1)}, bf16[8,24,1024]{2,1,0:T(8,128)(2,1)}, u32[]{:S(2)}, u32[]{:S(2)}) collective-permute-start(bf16[8,24,1024]{2,1,0:T(8,128)(2,1)S(1)} %all-to-all-done.here), channel_id=1, source_target_pairs={{0,1},{1,2},{2,3},{3,0},{4,5},{5,6},{6,7},{7,4},{8,9},{9,10},{10,1... | collective-permute-start | bytes 1179656 | tf_op jit(solution)/shard_map/ppermute | solution.py:24
  58.3 105.1 %copy-start.4 = (bf16[8,40,1024]{2,1,0:T(8,128)(2,1)}, bf16[8,40,1024]{2,1,0:T(8,128)(2,1)S(1)}, u32[]{:S(2)}) copy-start(bf16[8,40,1024]{2,1,0:T(8,128)(2,1)S(1)} %all-to-all-done.2.here) | copy-start | bytes 1966084
  58.3 105.1 %collective-permute-start.6 = (bf16[8,40,1024]{2,1,0:T(8,128)(2,1)S(1)}, bf16[8,40,1024]{2,1,0:T(8,128)(2,1)}, u32[]{:S(2)}, u32[]{:S(2)}) collective-permute-start(bf16[8,40,1024]{2,1,0:T(8,128)(2,1)S(1)} %all-to-all-done.2.here), channel_id=1, source_target_pairs={{0,3},{1,0},{2,1},{3,2},{4,7},{5,4},{6,5},{7,6},{8,11},{9,8},{10,9... | collective-permute-start | bytes 1966088 | tf_op jit(solution)/shard_map/ppermute | solution.py:24
  62.9 106.4 %collective-permute-start.5 = (bf16[8,40,1024]{2,1,0:T(8,128)(2,1)S(1)}, bf16[8,40,1024]{2,1,0:T(8,128)(2,1)}, u32[]{:S(2)}, u32[]{:S(2)}) collective-permute-start(bf16[8,40,1024]{2,1,0:T(8,128)(2,1)S(1)} %all-to-all-done.2.here), channel_id=1, source_target_pairs={{0,1},{1,2},{2,3},{3,0},{4,5},{5,6},{6,7},{7,4},{8,9},{9,10},{10,1... | collective-permute-start | bytes 1966088 | tf_op jit(solution)/shard_map/ppermute | solution.py:24
  97.6 16.9 %collective-permute-start.3 = (bf16[4,24,1024]{2,1,0:T(8,128)(2,1)}, bf16[4,24,1024]{2,1,0:T(8,128)(2,1)}, u32[]{:S(2)}, u32[]{:S(2)}) collective-permute-start(bf16[4,24,1024]{2,1,0:T(8,128)(2,1)} %slice.79), channel_id=1, source_target_pairs={{0,3},{1,0},{2,1},{3,2},{4,7},{5,4},{6,5},{7,6},{8,11},{9,8},{10,9... | collective-permute-start | bytes 589832 | tf_op jit(solution)/shard_map/ppermute | solution.py:24
  102.0 12.5 %collective-permute-start.2 = (bf16[4,24,1024]{2,1,0:T(8,128)(2,1)}, bf16[4,24,1024]{2,1,0:T(8,128)(2,1)}, u32[]{:S(2)}, u32[]{:S(2)}) collective-permute-start(bf16[4,24,1024]{2,1,0:T(8,128)(2,1)} %slice.78), channel_id=1, source_target_pairs={{0,1},{1,2},{2,3},{3,0},{4,5},{5,6},{6,7},{7,4},{8,9},{9,10},{10,1... | collective-permute-start | bytes 589832 | tf_op jit(solution)/shard_map/ppermute | solution.py:24
  106.3 167.0 %all-to-all-start.4 = ((bf16[32,16,128]{2,1,0:T(8,128)(2,1)}), bf16[32,16,128]{2,1,0:T(8,128)(2,1)S(1)}, u32[]{:S(2)}, u32[]{:S(2)}) async-start(bf16[32,16,128]{2,1,0:T(8,128)(2,1)} %bitcast.18), calls=%async_computation.4 | async-start | bytes 262144 | tf_op jit(solution)/shard_map/all_to_all | solution.py:106
  164.4 14.2 %collective-permute-start.8 = (bf16[4,40,1024]{2,1,0:T(8,128)(2,1)S(1)}, bf16[4,40,1024]{2,1,0:T(8,128)(2,1)S(1)}, u32[]{:S(2)}, u32[]{:S(2)}) collective-permute-start(bf16[4,40,1024]{2,1,0:T(8,128)(2,1)S(1)} %slice.81), channel_id=1, source_target_pairs={{0,3},{1,0},{2,1},{3,2},{4,7},{5,4},{6,5},{7,6},{8,11},{9,8},{10,9... | collective-permute-start | bytes 983048 | tf_op jit(solution)/shard_map/ppermute | solution.py:24
  170.3 11.7 %collective-permute-start.7 = (bf16[4,40,1024]{2,1,0:T(8,128)(2,1)S(1)}, bf16[4,40,1024]{2,1,0:T(8,128)(2,1)S(1)}, u32[]{:S(2)}, u32[]{:S(2)}) collective-permute-start(bf16[4,40,1024]{2,1,0:T(8,128)(2,1)S(1)} %slice.80), channel_id=1, source_target_pairs={{0,1},{1,2},{2,3},{3,0},{4,5},{5,6},{6,7},{7,4},{8,9},{9,10},{10,1... | collective-permute-start | bytes 983048 | tf_op jit(solution)/shard_map/ppermute | solution.py:24
  176.7 94.5 %collective-permute-start.4 = (bf16[384,896]{1,0:T(8,128)(2,1)}, bf16[384,896]{1,0:T(8,128)(2,1)}, u32[]{:S(2)}, u32[]{:S(2)}) collective-permute-start(bf16[384,896]{1,0:T(8,128)(2,1)} %bitcast.4), channel_id=1, source_target_pairs={{0,32},{32,0},{64,96},{96,64},{128,160},{160,128},{192,224},{224,1... | collective-permute-start | bytes 2064392 | tf_op jit(solution)/shard_map/ppermute | solution.py:118
  269.3 42.0 %collective-permute-start.9 = (bf16[640,896]{1,0:T(8,128)(2,1)}, bf16[640,896]{1,0:T(8,128)(2,1)}, u32[]{:S(2)}, u32[]{:S(2)}) collective-permute-start(bf16[640,896]{1,0:T(8,128)(2,1)} %bitcast.10), channel_id=1, source_target_pairs={{0,32},{32,0},{64,96},{96,64},{128,160},{160,128},{192,224},{224,1... | collective-permute-start | bytes 3440648 | tf_op jit(solution)/shard_map/ppermute | solution.py:118
  273.3 40.6 %all-to-all-start.1 = ((bf16[8,48,896]{2,1,0:T(8,128)(2,1)}), bf16[8,48,896]{2,1,0:T(8,128)(2,1)}, u32[]{:S(2)}, u32[]{:S(2)}) async-start(bf16[8,48,896]{2,1,0:T(8,128)(2,1)} %bitcast.49), calls=%async_computation.1 | async-start | bytes 1376256 | tf_op jit(solution)/shard_map/all_to_all | solution.py:120
  313.9 46.2 %all-to-all-start.3 = ((bf16[8,80,896]{2,1,0:T(8,128)(2,1)}), bf16[8,80,896]{2,1,0:T(8,128)(2,1)}, u32[]{:S(2)}, u32[]{:S(2)}) async-start(bf16[8,80,896]{2,1,0:T(8,128)(2,1)} %bitcast.46), calls=%async_computation.3 | async-start | bytes 2293760 | tf_op jit(solution)/shard_map/all_to_all | solution.py:120
  324.2 5.5 %collective-permute-start.10 = (f32[2,1024]{1,0:T(2,128)S(1)}, f32[2,1024]{1,0:T(2,128)S(1)}, u32[]{:S(2)}, u32[]{:S(2)}) collective-permute-start(f32[2,1024]{1,0:T(2,128)S(1)} %pad_maximum_fusion.1), channel_id=1, source_target_pairs={{0,1},{1,0},{2,3},{3,2},{4,5},{5,4},{6,7},{7,6},{8,9},{9,8},{10,11... | collective-permute-start | bytes 24584 | tf_op jit(solution)/shard_map/ppermute | solution.py:137
  329.7 7.0 %collective-permute-start.11 = (f32[2,1024]{1,0:T(2,128)S(1)}, f32[2,1024]{1,0:T(2,128)S(1)}, u32[]{:S(2)}, u32[]{:S(2)}) collective-permute-start(f32[2,1024]{1,0:T(2,128)S(1)} %fusion.38), channel_id=1, source_target_pairs={{0,2},{1,3},{2,0},{3,1},{4,6},{5,7},{6,4},{7,5},{8,10},{9,11},{10,... | collective-permute-start | bytes 24584 | tf_op jit(solution)/shard_map/ppermute | solution.py:137
  336.8 5.5 %collective-permute-start.12 = (f32[2,1024]{1,0:T(2,128)S(1)}, f32[2,1024]{1,0:T(2,128)S(1)}, u32[]{:S(2)}, u32[]{:S(2)}) collective-permute-start(f32[2,1024]{1,0:T(2,128)S(1)} %fusion.56), channel_id=1, source_target_pairs={{0,4},{1,5},{2,6},{3,7},{4,0},{5,1},{6,2},{7,3},{8,12},{9,13},{10,... | collective-permute-start | bytes 24584 | tf_op jit(solution)/shard_map/ppermute | solution.py:137
  342.4 6.4 %collective-permute-start.13 = (f32[2,1024]{1,0:T(2,128)S(1)}, f32[2,1024]{1,0:T(2,128)S(1)}, u32[]{:S(2)}, u32[]{:S(2)}) collective-permute-start(f32[2,1024]{1,0:T(2,128)S(1)} %add.106), channel_id=1, source_target_pairs={{0,8},{1,9},{2,10},{3,11},{4,12},{5,13},{6,14},{7,15},{8,0},{9,1},... | collective-permute-start | bytes 24584 | tf_op jit(solution)/shard_map/ppermute | solution.py:137
  348.8 9.4 %collective-permute-start.14 = (f32[2,1024]{1,0:T(2,128)S(1)}, f32[2,1024]{1,0:T(2,128)S(1)}, u32[]{:S(2)}, u32[]{:S(2)}) collective-permute-start(f32[2,1024]{1,0:T(2,128)S(1)} %add.107), channel_id=1, source_target_pairs={{0,16},{1,17},{2,18},{3,19},{4,20},{5,21},{6,22},{7,23},{8,24},{9,... | collective-permute-start | bytes 24584 | tf_op jit(solution)/shard_map/ppermute | solution.py:137
  (15 other events, 171.9 us)
Sparse Core Ops, SparseCore 0:
  41.4 83.3 all-gather.1

commit v2 on v1

v2 whole, which is shorter than its diff:
```python
import math

import jax
import jax.numpy as jnp
from jax import lax
from jax.experimental import pallas as pl
from jax.experimental.pallas import tpu as pltpu
from jax.sharding import PartitionSpec as P


first_fix = 1.0 - math.exp(1000.0 * math.log(0.9))
second_fix = 1.0 - math.exp(1000.0 * math.log(0.999))

BF = jnp.bfloat16
F32 = jnp.float32
TOK = ("dp", "row")
Z_GROUPS = [[4 * z + x for z in range(8)] for x in range(4)]
Y_GROUPS = [[2 * m + q for m in range(8)] for q in range(2)]
PAIR = [(k, k ^ 1) for k in range(16)]


def along_x(value, step):
    return lax.ppermute(value, "col", [(c, c - c % 4 + (c % 4 + step) % 4) for c in range(32)])


def activation(gate_pre, up_pre):
    gate_f = gate_pre.astype(F32)
    sigma = jax.nn.sigmoid(gate_f)
    return gate_f, sigma, gate_f * sigma, up_pre.astype(F32)


def dot_nt(left, right):
    return lax.dot_general(left, right, (((1,), (1,)), ((), ())), preferred_element_type=F32)


def dot_tn(left, right):
    return lax.dot_general(left, right, (((0,), (0,)), ((), ())), preferred_element_type=F32)


def along_y(value, step):
    def index(y, core):
        return 2 * (4 * (y % 2) + y // 2) + core

    return lax.ppermute(value, TOK, [(index(y, q), index((y + step) % 8, q)) for y in range(8) for q in range(2)])


def place_out_kernel(here_ref, here, left, right, far_low, far_high, own, other):
    x, core = here_ref[0], here_ref[1]
    half = far_low.shape[0]
    for back, parts in ((0, ((here, 0),)), (1, ((left, 0),)), (3, ((right, 0),)), (2, ((far_low, 0), (far_high, half)))):
        source = lax.rem(x + 4 - back, 4)
        mine = source // 2 == core
        for piece, first in parts:
            rows = pl.ds(first, piece.shape[0])

            @pl.when(mine)
            def _():
                own[rows, source % 2] = piece[...]

            @pl.when(jnp.logical_not(mine))
            def _():
                other[rows, source % 2] = piece[...]


def place_out(where, pieces):
    planes, rows, width = pieces[0].shape
    return pl.pallas_call(
        place_out_kernel,
        out_shape=[jax.ShapeDtypeStruct((planes, 2, rows, width), BF)] * 2,
        in_specs=[pl.BlockSpec(memory_space=pltpu.SMEM)] + [pl.BlockSpec(memory_space=pltpu.VMEM)] * 5,
        out_specs=[pl.BlockSpec(memory_space=pltpu.VMEM)] * 2,
        name="place_out",
    )(where, *pieces)


def place_hid_kernel(y_ref, *refs):
    pieces, out = refs[:-1], refs[-1]
    y = y_ref[0]
    half = pieces[-1].shape[0]
    for back, piece, first in (
        *((d, pieces[d], 0) for d in range(4)),
        *((8 - d, pieces[3 + d], 0) for d in range(1, 4)),
        (4, pieces[7], 0),
        (4, pieces[8], half),
    ):
        source = lax.rem(y + 8 - back, 8)
        m = 4 * (source % 2) + source // 2
        out[m, pl.ds(first, piece.shape[0])] = piece[...]


def place_hid(y, pieces):
    rows, units = pieces[0].shape
    return pl.pallas_call(
        place_hid_kernel,
        out_shape=jax.ShapeDtypeStruct((8, rows, units), BF),
        in_specs=[pl.BlockSpec(memory_space=pltpu.SMEM)] + [pl.BlockSpec(memory_space=pltpu.VMEM)] * 9,
        out_specs=pl.BlockSpec(memory_space=pltpu.VMEM),
        name="place_hid",
    )(y[None], *pieces)


def gather_out(value, where):
    sent = jnp.broadcast_to(value[None], (8,) + value.shape).reshape((-1,) + value.shape[1:])
    here = lax.all_to_all(sent, "col", 0, 0, tiled=True, axis_index_groups=Z_GROUPS)
    here = here.reshape((8,) + value.shape)
    left = along_x(here, 1)
    right = along_x(here, -1)
    far_low = along_x(left[:4], 1)
    far_high = along_x(right[4:], -1)
    return place_out(where, (here, left, right, far_low, far_high))


def gather_hid(value, y):
    up, down = [value], [value]
    for _ in range(1, 4):
        up.append(along_y(up[-1], 1))
        down.append(along_y(down[-1], -1))
    half = value.shape[0] // 2
    far_low = along_y(up[3][:half], 1)
    far_high = along_y(down[3][half:], -1)
    return place_hid(y, (*up, *down[1:], far_low, far_high))


def exact(left, right):
    high = left.astype(BF)
    rest = left - high.astype(F32)
    mid = rest.astype(BF)
    low = (rest - mid.astype(F32)).astype(BF)
    terms = lax.dot_general(
        jnp.concatenate([high, mid, low], axis=0), right, (((1,), (0,)), ((), ())), preferred_element_type=F32
    ).reshape(3, 16, right.shape[1])
    return terms[0] + (terms[1] + terms[2])


def work(gate_pre, up_pre, grad_out, down_weight, basis, first_moment_in, second_moment_in):
    width = grad_out.shape[1]
    units = gate_pre.shape[1]
    core = lax.axis_index("row") % 2
    y = 2 * (lax.axis_index("row") // 2) + lax.axis_index("dp")
    x = lax.axis_index("col") % 4

    out_own, out_other = gather_out(grad_out, jnp.stack([x, core]))
    out_own, out_other = out_own.reshape(1024, width), out_other.reshape(1024, width)

    _, _, act_early, up_early = activation(gate_pre, up_pre)
    hidden = (act_early * up_early).astype(BF)
    both = jnp.concatenate([hidden, basis], axis=0)
    both_own = gather_hid(both, y)
    both_other = lax.ppermute(both_own, TOK, PAIR)
    hidden_own, hidden_other = (v[:, :128].reshape(1024, units) for v in (both_own, both_other))

    tp_own, tp_other = (
        dot_nt(v[:, 128:].reshape(256, units), hidden).astype(BF).reshape(8, 1, 32, 128) for v in (both_own, both_other)
    )
    tp_part = jnp.where(
        core == 0,
        jnp.concatenate([tp_own, tp_other], axis=1),
        jnp.concatenate([tp_other, tp_own], axis=1),
    ).reshape(512, 128)
    tp_got = lax.all_to_all(tp_part, "col", 0, 0, tiled=True).reshape(32, 16, 128)
    tp_mine = jnp.sum(tp_got.astype(F32), axis=0)
    tp_sent = jnp.broadcast_to(tp_mine[None], (16, 16, 128)).reshape(256, 128)
    tp_all = lax.all_to_all(tp_sent, TOK, 0, 0, tiled=True).reshape(8, 2, 16, 128)

    def tp_rows(which):
        return lax.dynamic_index_in_dim(tp_all, which, 1, keepdims=False).transpose(1, 0, 2).reshape(16, 1024)

    part_other = dot_nt(out_other, down_weight).astype(BF)
    part_got = lax.ppermute(part_other, TOK, PAIR)
    part_sum = (dot_nt(out_own, down_weight) + part_got.astype(F32)).astype(BF)
    blocks = lax.all_to_all(part_sum, TOK, 0, 0, tiled=True, axis_index_groups=Y_GROUPS)
    summed = jnp.sum(blocks.reshape(8, 128, units).astype(F32), axis=0).astype(BF)
    gate_late, up_late, summed = lax.optimization_barrier((gate_pre, up_pre, summed))
    gate_f, sigma, act_value, up_f = activation(gate_late, up_late)
    grad_hidden = summed.astype(F32)
    grad_up = (grad_hidden * act_value).astype(BF)
    grad_gate = (grad_hidden * up_f * sigma * (1.0 + gate_f * (1.0 - sigma))).astype(BF)

    projected = exact(tp_rows(core), out_own) + exact(tp_rows(1 - core), out_other)
    first_moment = 0.9 * first_moment_in + 0.1 * projected
    second_moment = 0.999 * second_moment_in + 0.001 * projected * projected
    adapted = first_moment / first_fix / (jnp.sqrt(second_moment / second_fix) + 1e-06)
    totals = jnp.stack([jnp.sum(adapted * adapted, axis=0), jnp.sum(projected * projected, axis=0)])
    for bit in (1, 2, 4, 8, 16):
        totals = totals + lax.ppermute(totals, "col", [(c, c ^ bit) for c in range(32)])
    column_scale = jnp.sqrt(totals[0]) / (jnp.sqrt(totals[1]) + 1e-06)

    terms = (dot_tn(hidden_own, out_own), dot_tn(hidden_other, out_other))
    grad_weight = sum(terms).astype(BF)
    scaled_grad = (grad_weight.astype(F32) * column_scale[None, :]).astype(BF)
    return (grad_gate, grad_up, scaled_grad, first_moment, second_moment)


def solution(mesh):
    rows = P(TOK, "col")
    cols = P("col", TOK)
    return jax.shard_map(
        work,
        mesh=mesh,
        in_specs=(rows, rows, cols, cols, rows, cols, cols),
        out_specs=(rows, rows, cols, cols, cols),
        check_vma=False,
    )
```

time: 382 us -> 210 us (0.55)
  Pallas kernels: 129 us -> 7.65 us
  blocking collectives: 64.7 us -> 14.4 us
  waiting for transfers between devices: 44.3 us -> 69.8 us
  between operations: 14.6 us -> 1.17 us
  other arithmetic: 13.3 us -> 5.39 us
  local copies, waits for them, and re-layouts: 18.4 us -> 13.4 us
    pallas_call x2, Pallas kernels: 129 us -> 7.65 us  [the longest x1 4.52 us: place_out(): pl.pallas_call(place_out_kernel, out_shape=[jax.ShapeDtypeStruct((planes,...]
    all_gather x2 -> x0, blocking collectives: 64.7 us -> none  [the longest x1 32.8 us: work(): lax.all_gather(tp_mine, TOK, axis=1, tiled=True).reshape(16, 32, 64)]
    ppermute x0 -> x9, starting transfers between devices: none -> 24.7 us  [the longest x8 22.8 us: along_y(): lax.ppermute(value, TOK, [(index(y, q), index((y + step) % 8, q)) for y i...]
    ppermute x0 -> x9, waiting for transfers between devices: none -> 16.2 us  [the longest x8 16.2 us: along_y(): lax.ppermute(value, TOK, [(index(y, q), index((y + step) % 8, q)) for y i...]
    all_to_all x0 -> x1, blocking collectives: none -> 14.4 us  [work(): lax.all_to_all(tp_part, 'col', 0, 0, tiled=True).reshape(32, 16, 128)]
    ppermute x8 -> x4, starting transfers between devices: 25.9 us -> 13.3 us  [along_x(): lax.ppermute(value, 'col', [(c, c - c % 4 + (c % 4 + step) % 4) for c in...]
    ppermute x8 -> x4, waiting for transfers between devices: 3.37 us -> 14.6 us  [along_x(): lax.ppermute(value, 'col', [(c, c - c % 4 + (c % 4 + step) % 4) for c in...]
    all_to_all x3 -> x2, waiting for transfers between devices: 25.9 us -> 18.9 us  [the longest x1 11.4 us: gather_out(): lax.all_to_all(sent, 'col', 0, 0, tiled=True, axis_index_groups=Z_GROUPS)]
  transfers between devices with their start and end apart: 21 -> 22, of which waited for: 8 -> 14; matrix products, arithmetic and copies ran while one was open for 9% -> 12% of each run, Pallas kernels for 34% -> 4%
where the time goes in v2:
time: 210 us; the launch traced here: 209 us
  starting transfers between devices  77 us (37%)
  waiting for transfers between devices  69.8 us (33%)
  matrix products  19.9 us (9%)
  blocking collectives  14.4 us (7%)
  local copies, waits for them, and re-layouts  13.4 us (6%)
  Pallas kernels  7.65 us (4%)
  other arithmetic  5.39 us (3%)
    ppermute x8, starting transfers between devices, along_y(): lax.ppermute(value, TOK, [(index(y, q), index((y + step) % 8, q)) for y i...  22.8 us
    ppermute x8, waiting for transfers between devices, along_y(): lax.ppermute(value, TOK, [(index(y, q), index((y + step) % 8, q)) for y i...  16.2 us
    ppermute x5, waiting for transfers between devices, work(): lax.ppermute(totals, 'col', [(c, c ^ bit) for c in range(32)])  16.1 us
    ppermute x4, waiting for transfers between devices, along_x(): lax.ppermute(value, 'col', [(c, c - c % 4 + (c % 4 + step) % 4) for c in...  14.6 us
    all_to_all x1, blocking collectives, work(): lax.all_to_all(tp_part, 'col', 0, 0, tiled=True).reshape(32, 16, 128)  14.4 us
    ppermute x5, starting transfers between devices, work(): lax.ppermute(totals, 'col', [(c, c ^ bit) for c in range(32)])  13.8 us
    ppermute x4, starting transfers between devices, along_x(): lax.ppermute(value, 'col', [(c, c - c % 4 + (c % 4 + step) % 4) for c in...  13.3 us
    dot_general x4, matrix products, dot_nt(): lax.dot_general(left, right, (((1,), (1,)), ((), ())), preferred_element_...  11.5 us
  transfers between devices with their start and end apart: 22, of which 14 were waited for; matrix products, arithmetic and copies ran while one was open for 12% of the time, Pallas kernels for 4%

profile of v2, /device:TPU:8, one launch (start us, length us, event | category | flops | bytes accessed | tf_op | source)
XLA Modules:
  0.0 208.7 jit_solution(15125107446963745719)
XLA Ops:
  2.8 10.3 %all-to-all-start = ((bf16[8,64,1024]{2,1,0:T(8,128)(2,1)}), bf16[8,64,1024]{2,1,0:T(8,128)(2,1)S(1)}, u32[]{:S(2)}, u32[]{:S(2)}) async-start(bf16[8,64,1024]{2,1,0:T(8,128)(2,1)} %broadcast_in_dim.6), calls=%async_computation | async-start | bytes 2097152 | tf_op jit(solution)/shard_map/all_to_all | solution.py:104
  16.6 3.5 %collective-permute-start.5 = (bf16[160,896]{1,0:T(8,128)(2,1)S(1)}, bf16[160,896]{1,0:T(8,128)(2,1)}, u32[]{:S(2)}, u32[]{:S(2)}) collective-permute-start(bf16[160,896]{1,0:T(8,128)(2,1)S(1)} %pad_maximum_fusion.refs_0_), channel_id=1, source_target_pairs={{0,256},{32,288},{256,64},{288,96},{64,320},{96,352},{320,128},{35... | collective-permute-start | bytes 860168 | tf_op jit(solution)/shard_map/ppermute | solution.py:44
  20.1 4.4 %collective-permute-done.8.refs_4_ = bf16[160,896]{1,0:T(8,128)(2,1)} collective-permute-done((bf16[160,896]{1,0:T(8,128)(2,1)S(1)}, bf16[160,896]{1,0:T(8,128)(2,1)}, u32[]{:S(2)}, u32[]{:S(2)}) %collective-permute-start.8) | collective-permute-done | bytes 286752 | tf_op jit(solution)/shard_map/ppermute | solution.py:44
  30.4 11.4 %all-to-all-done.here = bf16[8,64,1024]{2,1,0:T(8,128)(2,1)S(1)} async-done(((bf16[8,64,1024]{2,1,0:T(8,128)(2,1)}), bf16[8,64,1024]{2,1,0:T(8,128)(2,1)S(1)}, u32[]{:S(2)}, u32[]{:S(2)}) %all-to-all-start) | async-done | bytes 1048608 | tf_op jit(solution)/shard_map/all_to_all | solution.py:104
  41.9 4.7 %collective-permute-start.1 = (bf16[8,64,1024]{2,1,0:T(8,128)(2,1)S(1)}, bf16[8,64,1024]{2,1,0:T(8,128)(2,1)}, u32[]{:S(2)}, u32[]{:S(2)}) collective-permute-start(bf16[8,64,1024]{2,1,0:T(8,128)(2,1)S(1)} %all-to-all-done.here), channel_id=1, source_target_pairs={{0,3},{1,0},{2,1},{3,2},{4,7},{5,4},{6,5},{7,6},{8,11},{9,8},{10,9... | collective-permute-start | bytes 3145736 | tf_op jit(solution)/shard_map/ppermute | solution.py:23
  50.8 3.5 %collective-permute-start.7 = (bf16[160,896]{1,0:T(8,128)(2,1)}, bf16[160,896]{1,0:T(8,128)(2,1)S(1)}, u32[]{:S(2)}, u32[]{:S(2)}) collective-permute-start(bf16[160,896]{1,0:T(8,128)(2,1)} %collective-permute-done.6.refs_2_), channel_id=1, source_target_pairs={{0,256},{32,288},{256,64},{288,96},{64,320},{96,352},{320,128},{35... | collective-permute-start | bytes 860168 | tf_op jit(solution)/shard_map/ppermute | solution.py:44
  54.3 4.7 %collective-permute-done.10.refs_6_ = bf16[160,896]{1,0:T(8,128)(2,1)S(1)} collective-permute-done((bf16[160,896]{1,0:T(8,128)(2,1)}, bf16[160,896]{1,0:T(8,128)(2,1)S(1)}, u32[]{:S(2)}, u32[]{:S(2)}) %collective-permute-start.10) | collective-permute-done | bytes 286752 | tf_op jit(solution)/shard_map/ppermute | solution.py:44
  60.4 3.4 %collective-permute-start.12 = (bf16[80,896]{1,0:T(8,128)(2,1)}, bf16[80,896]{1,0:T(8,128)(2,1)S(1)}, u32[]{:S(2)}, u32[]{:S(2)}) collective-permute-start(bf16[80,896]{1,0:T(8,128)(2,1)} %slice.73), channel_id=1, source_target_pairs={{0,448},{32,480},{256,0},{288,32},{64,256},{96,288},{320,64},{352,... | collective-permute-start | bytes 430088 | tf_op jit(solution)/shard_map/ppermute | solution.py:44
  67.7 6.4 %collective-permute-done.11.refs_7_ = bf16[80,896]{1,0:T(8,128)(2,1)} collective-permute-done((bf16[80,896]{1,0:T(8,128)(2,1)}, bf16[80,896]{1,0:T(8,128)(2,1)}, u32[]{:S(2)}, u32[]{:S(2)}) %collective-permute-start.11) | collective-permute-done | bytes 143392 | tf_op jit(solution)/shard_map/ppermute | solution.py:44
  81.1 4.8 %collective-permute-start.3 = (bf16[4,64,1024]{2,1,0:T(8,128)(2,1)}, bf16[4,64,1024]{2,1,0:T(8,128)(2,1)}, u32[]{:S(2)}, u32[]{:S(2)}) collective-permute-start(bf16[4,64,1024]{2,1,0:T(8,128)(2,1)} %slice.71), channel_id=1, source_target_pairs={{0,3},{1,0},{2,1},{3,2},{4,7},{5,4},{6,5},{7,6},{8,11},{9,8},{10,9... | collective-permute-start | bytes 1572872 | tf_op jit(solution)/shard_map/ppermute | solution.py:23
  89.6 8.5 %collective-permute-done.3.far_high = bf16[4,64,1024]{2,1,0:T(8,128)(2,1)} collective-permute-done((bf16[4,64,1024]{2,1,0:T(8,128)(2,1)}, bf16[4,64,1024]{2,1,0:T(8,128)(2,1)}, u32[]{:S(2)}, u32[]{:S(2)}) %collective-permute-start.3) | collective-permute-done | bytes 524320 | tf_op jit(solution)/shard_map/ppermute | solution.py:23
  98.1 6.1 %collective-permute-done.2.far_low = bf16[4,64,1024]{2,1,0:T(8,128)(2,1)S(1)} collective-permute-done((bf16[4,64,1024]{2,1,0:T(8,128)(2,1)S(1)}, bf16[4,64,1024]{2,1,0:T(8,128)(2,1)S(1)}, u32[]{:S(2)}, u32[]{:S(2)}) %collective-permute-start.2) | collective-permute-done | bytes 524320 | tf_op jit(solution)/shard_map/ppermute | solution.py:23
  105.0 4.5 %place_out.1 = (bf16[8,2,64,1024]{3,2,1,0:T(8,128)(2,1)}, bf16[8,2,64,1024]{3,2,1,0:T(8,128)(2,1)}) custom-call(s32[2]{0:T(128)} %pad_add_fusion.here_ref, bf16[8,64,1024]{2,1,0:T(8,128)(2,1)} %copy-done.2, bf16[8,64,1024]{2,1,0:T(8,128)(2,1)} %collective-permute-done.left, bf16[8,64,1024]{2,1,0:T(8,128)(2,1)} %collective-permute-done.1.right, ...), custom_call_target="tpu_custom_call" | custom-call | tf_op jit(solution)/shard_map/place_out/pallas_call | solution.py:67
  109.5 5.2 %convolution_convert_fusion = bf16[1024,896]{1,0:T(8,128)(2,1)} fusion(bf16[1024,1024]{1,0:T(8,128)(2,1)} %bitcast.76, bf16[896,1024]{1,0:T(8,128)(2,1)S(1)} %copy-done), kind=kOutput, calls=%fused_computation.3 | convolution fusion | flops 1879965696 | bytes 5767168 | tf_op jit(solution)/shard_map/dot_general | solution.py:33
  119.4 14.4 %all_to_all.27 = bf16[32,16,128]{2,1,0:T(8,128)(2,1)S(1)} all-to-all(bf16[32,16,128]{2,1,0:T(8,128)(2,1)S(1)} %bitcast.85), channel_id=1, replica_groups=mesh['dp'=2,'row'=8,'col'=32] {'col'}, dimensions={0} | all-to-all | bytes 262144 | tf_op jit(solution)/shard_map/all_to_all | solution.py:160
  134.5 7.3 %all-to-all-start.3 = ((f32[16,16,128]{2,1,0:T(8,128)}), f32[16,16,128]{2,1,0:T(8,128)S(1)}, u32[]{:S(2)}, u32[]{:S(2)}) async-start(f32[16,16,128]{2,1,0:T(8,128)} %broadcast_in_dim.8), calls=%async_computation.3 | async-start | bytes 262144 | tf_op jit(solution)/shard_map/all_to_all | solution.py:163
  141.8 7.5 %all-to-all-done.3 = f32[16,16,128]{2,1,0:T(8,128)S(1)} async-done(((f32[16,16,128]{2,1,0:T(8,128)}), f32[16,16,128]{2,1,0:T(8,128)S(1)}, u32[]{:S(2)}, u32[]{:S(2)}) %all-to-all-start.3) | async-done | bytes 131104 | tf_op jit(solution)/shard_map/all_to_all | solution.py:163
  149.3 5.7 %add_convert_fusion.1 = bf16[1024,896]{1,0:T(8,128)(2,1)} fusion(bf16[1024,896]{1,0:T(8,128)(2,1)} %collective-permute-done.4, bf16[1024,1024]{1,0:T(8,128)(2,1)} %bitcast.73, bf16[896,1024]{1,0:T(8,128)(2,1)S(1)} %copy-done), kind=kOutput, calls=%fused_computation.2 | convolution fusion | flops 1881800704 | bytes 7602176 | tf_op jit(solution)/shard_map/dot_general | solution.py:33
  155.1 5.7 %all-to-all-start.1 = ((bf16[8,128,896]{2,1,0:T(8,128)(2,1)}), bf16[8,128,896]{2,1,0:T(8,128)(2,1)}, u32[]{:S(2)}, u32[]{:S(2)}) async-start(bf16[8,128,896]{2,1,0:T(8,128)(2,1)} %bitcast.79), calls=%async_computation.1 | async-start | bytes 3670016 | tf_op jit(solution)/shard_map/all_to_all | solution.py:171
  166.3 3.6 %collective-permute-done.14 = f32[2,1024]{1,0:T(2,128)S(1)} collective-permute-done((f32[2,1024]{1,0:T(2,128)S(1)}, f32[2,1024]{1,0:T(2,128)S(1)}, u32[]{:S(2)}, u32[]{:S(2)}) %collective-permute-start.14) | collective-permute-done | bytes 8224 | tf_op jit(solution)/shard_map/ppermute | solution.py:185
  173.0 3.9 %collective-permute-done.15 = f32[2,1024]{1,0:T(2,128)S(1)} collective-permute-done((f32[2,1024]{1,0:T(2,128)S(1)}, f32[2,1024]{1,0:T(2,128)S(1)}, u32[]{:S(2)}, u32[]{:S(2)}) %collective-permute-start.15) | collective-permute-done | bytes 8224 | tf_op jit(solution)/shard_map/ppermute | solution.py:185
  194.3 4.1 %collective-permute-done.18 = f32[2,1024]{1,0:T(2,128)S(1)} collective-permute-done((f32[2,1024]{1,0:T(2,128)S(1)}, f32[2,1024]{1,0:T(2,128)S(1)}, u32[]{:S(2)}, u32[]{:S(2)}) %collective-permute-start.18) | collective-permute-done | bytes 8224 | tf_op jit(solution)/shard_map/ppermute | solution.py:185
  198.4 3.5 %multiply_convert_fusion = bf16[896,1024]{1,0:T(8,128)(2,1)} fusion(f32[896,1024]{1,0:T(8,128)S(1)} %fusion.38, f32[1024]{0:T(1024)S(1)} %bitcast.94, bf16[1024,896]{1,0:T(8,128)(2,1)S(1)} %bitcast.80, bf16[1024,1024]{1,0:T(8,128)(2,1)S(1)} %bitcast.75), kind=kOutput, calls=%fused_computation | convolution fusion | flops 1883635712 | bytes 9441280 | tf_op jit(solution)/shard_map/dot_general | solution.py:37
  202.0 4.0 %all-to-all-done.1 = bf16[8,128,896]{2,1,0:T(8,128)(2,1)} async-done(((bf16[8,128,896]{2,1,0:T(8,128)(2,1)}), bf16[8,128,896]{2,1,0:T(8,128)(2,1)}, u32[]{:S(2)}, u32[]{:S(2)}) %all-to-all-start.1) | async-done | bytes 1835040 | tf_op jit(solution)/shard_map/all_to_all | solution.py:171
  (92 shorter events, 66.3 us)
Async XLA Ops:
  0.6 108.9 %copy-start = (bf16[896,1024]{1,0:T(8,128)(2,1)S(1)}, bf16[896,1024]{1,0:T(8,128)(2,1)}, u32[]{:S(2)}) copy-start(bf16[896,1024]{1,0:T(8,128)(2,1)} %param.10) | copy-start | bytes 5505028
  2.8 39.0 %all-to-all-start = ((bf16[8,64,1024]{2,1,0:T(8,128)(2,1)}), bf16[8,64,1024]{2,1,0:T(8,128)(2,1)S(1)}, u32[]{:S(2)}, u32[]{:S(2)}) async-start(bf16[8,64,1024]{2,1,0:T(8,128)(2,1)} %broadcast_in_dim.6), calls=%async_computation | async-start | bytes 2097152 | tf_op jit(solution)/shard_map/all_to_all | solution.py:104
  14.3 59.9 %copy-start.5 = (bf16[160,896]{1,0:T(8,128)(2,1)}, bf16[160,896]{1,0:T(8,128)(2,1)S(1)}, u32[]{:S(2)}) copy-start(bf16[160,896]{1,0:T(8,128)(2,1)S(1)} %pad_maximum_fusion.refs_0_) | copy-start | bytes 860164
  14.3 10.3 %collective-permute-start.8 = (bf16[160,896]{1,0:T(8,128)(2,1)S(1)}, bf16[160,896]{1,0:T(8,128)(2,1)}, u32[]{:S(2)}, u32[]{:S(2)}) collective-permute-start(bf16[160,896]{1,0:T(8,128)(2,1)S(1)} %pad_maximum_fusion.refs_0_), channel_id=1, source_target_pairs={{0,448},{32,480},{256,0},{288,32},{64,256},{96,288},{320,64},{352,... | collective-permute-start | bytes 860168 | tf_op jit(solution)/shard_map/ppermute | solution.py:44
  16.6 11.7 %collective-permute-start.5 = (bf16[160,896]{1,0:T(8,128)(2,1)S(1)}, bf16[160,896]{1,0:T(8,128)(2,1)}, u32[]{:S(2)}, u32[]{:S(2)}) collective-permute-start(bf16[160,896]{1,0:T(8,128)(2,1)S(1)} %pad_maximum_fusion.refs_0_), channel_id=1, source_target_pairs={{0,256},{32,288},{256,64},{288,96},{64,320},{96,352},{320,128},{35... | collective-permute-start | bytes 860168 | tf_op jit(solution)/shard_map/ppermute | solution.py:44
  24.6 23.9 %collective-permute-start.9 = (bf16[160,896]{1,0:T(8,128)(2,1)}, bf16[160,896]{1,0:T(8,128)(2,1)}, u32[]{:S(2)}, u32[]{:S(2)}) collective-permute-start(bf16[160,896]{1,0:T(8,128)(2,1)} %collective-permute-done.8.refs_4_), channel_id=1, source_target_pairs={{0,448},{32,480},{256,0},{288,32},{64,256},{96,288},{320,64},{352,... | collective-permute-start | bytes 860168 | tf_op jit(solution)/shard_map/ppermute | solution.py:44
  28.4 22.4 %collective-permute-start.6 = (bf16[160,896]{1,0:T(8,128)(2,1)}, bf16[160,896]{1,0:T(8,128)(2,1)}, u32[]{:S(2)}, u32[]{:S(2)}) collective-permute-start(bf16[160,896]{1,0:T(8,128)(2,1)} %collective-permute-done.5.refs_1_), channel_id=1, source_target_pairs={{0,256},{32,288},{256,64},{288,96},{64,320},{96,352},{320,128},{35... | collective-permute-start | bytes 860168 | tf_op jit(solution)/shard_map/ppermute | solution.py:44
  41.9 37.3 %collective-permute-start.1 = (bf16[8,64,1024]{2,1,0:T(8,128)(2,1)S(1)}, bf16[8,64,1024]{2,1,0:T(8,128)(2,1)}, u32[]{:S(2)}, u32[]{:S(2)}) collective-permute-start(bf16[8,64,1024]{2,1,0:T(8,128)(2,1)S(1)} %all-to-all-done.here), channel_id=1, source_target_pairs={{0,3},{1,0},{2,1},{3,2},{4,7},{5,4},{6,5},{7,6},{8,11},{9,8},{10,9... | collective-permute-start | bytes 3145736 | tf_op jit(solution)/shard_map/ppermute | solution.py:23
  46.5 39.4 %collective-permute-start = (bf16[8,64,1024]{2,1,0:T(8,128)(2,1)S(1)}, bf16[8,64,1024]{2,1,0:T(8,128)(2,1)}, u32[]{:S(2)}, u32[]{:S(2)}) collective-permute-start(bf16[8,64,1024]{2,1,0:T(8,128)(2,1)S(1)} %all-to-all-done.here), channel_id=1, source_target_pairs={{0,1},{1,2},{2,3},{3,0},{4,5},{5,6},{6,7},{7,4},{8,9},{9,10},{10,1... | collective-permute-start | bytes 3145736 | tf_op jit(solution)/shard_map/ppermute | solution.py:23
  48.5 10.6 %collective-permute-start.10 = (bf16[160,896]{1,0:T(8,128)(2,1)}, bf16[160,896]{1,0:T(8,128)(2,1)S(1)}, u32[]{:S(2)}, u32[]{:S(2)}) collective-permute-start(bf16[160,896]{1,0:T(8,128)(2,1)} %collective-permute-done.9.refs_5_), channel_id=1, source_target_pairs={{0,448},{32,480},{256,0},{288,32},{64,256},{96,288},{320,64},{352,... | collective-permute-start | bytes 860168 | tf_op jit(solution)/shard_map/ppermute | solution.py:44
  50.8 13.0 %collective-permute-start.7 = (bf16[160,896]{1,0:T(8,128)(2,1)}, bf16[160,896]{1,0:T(8,128)(2,1)S(1)}, u32[]{:S(2)}, u32[]{:S(2)}) collective-permute-start(bf16[160,896]{1,0:T(8,128)(2,1)} %collective-permute-done.6.refs_2_), channel_id=1, source_target_pairs={{0,256},{32,288},{256,64},{288,96},{64,320},{96,352},{320,128},{35... | collective-permute-start | bytes 860168 | tf_op jit(solution)/shard_map/ppermute | solution.py:44
  60.4 7.3 %collective-permute-start.12 = (bf16[80,896]{1,0:T(8,128)(2,1)}, bf16[80,896]{1,0:T(8,128)(2,1)S(1)}, u32[]{:S(2)}, u32[]{:S(2)}) collective-permute-start(bf16[80,896]{1,0:T(8,128)(2,1)} %slice.73), channel_id=1, source_target_pairs={{0,448},{32,480},{256,0},{288,32},{64,256},{96,288},{320,64},{352,... | collective-permute-start | bytes 430088 | tf_op jit(solution)/shard_map/ppermute | solution.py:44
  65.3 8.9 %collective-permute-start.11 = (bf16[80,896]{1,0:T(8,128)(2,1)}, bf16[80,896]{1,0:T(8,128)(2,1)}, u32[]{:S(2)}, u32[]{:S(2)}) collective-permute-start(bf16[80,896]{1,0:T(8,128)(2,1)} %slice.72), channel_id=1, source_target_pairs={{0,256},{32,288},{256,64},{288,96},{64,320},{96,352},{320,128},{35... | collective-permute-start | bytes 430088 | tf_op jit(solution)/shard_map/ppermute | solution.py:44
  77.3 40.7 %collective-permute-start.13 = (bf16[8,160,896]{2,1,0:T(8,128)(2,1)}, bf16[8,160,896]{2,1,0:T(8,128)(2,1)}, u32[]{:S(2)}, u32[]{:S(2)}) collective-permute-start(bf16[8,160,896]{2,1,0:T(8,128)(2,1)} %place_hid.1), channel_id=1, source_target_pairs={{0,32},{32,0},{64,96},{96,64},{128,160},{160,128},{192,224},{224,1... | collective-permute-start | bytes 6881288 | tf_op jit(solution)/shard_map/ppermute | solution.py:149
  81.1 17.0 %collective-permute-start.3 = (bf16[4,64,1024]{2,1,0:T(8,128)(2,1)}, bf16[4,64,1024]{2,1,0:T(8,128)(2,1)}, u32[]{:S(2)}, u32[]{:S(2)}) collective-permute-start(bf16[4,64,1024]{2,1,0:T(8,128)(2,1)} %slice.71), channel_id=1, source_target_pairs={{0,3},{1,0},{2,1},{3,2},{4,7},{5,4},{6,5},{7,6},{8,11},{9,8},{10,9... | collective-permute-start | bytes 1572872 | tf_op jit(solution)/shard_map/ppermute | solution.py:23
  87.0 17.2 %collective-permute-start.2 = (bf16[4,64,1024]{2,1,0:T(8,128)(2,1)S(1)}, bf16[4,64,1024]{2,1,0:T(8,128)(2,1)S(1)}, u32[]{:S(2)}, u32[]{:S(2)}) collective-permute-start(bf16[4,64,1024]{2,1,0:T(8,128)(2,1)S(1)} %slice.70), channel_id=1, source_target_pairs={{0,1},{1,2},{2,3},{3,0},{4,5},{5,6},{6,7},{7,4},{8,9},{9,10},{10,1... | collective-permute-start | bytes 1572872 | tf_op jit(solution)/shard_map/ppermute | solution.py:23
  114.7 34.6 %collective-permute-start.4 = (bf16[1024,896]{1,0:T(8,128)(2,1)}, bf16[1024,896]{1,0:T(8,128)(2,1)}, u32[]{:S(2)}, u32[]{:S(2)}) collective-permute-start(bf16[1024,896]{1,0:T(8,128)(2,1)} %convolution_convert_fusion), channel_id=1, source_target_pairs={{0,32},{32,0},{64,96},{96,64},{128,160},{160,128},{192,224},{224,1... | collective-permute-start | bytes 5505032 | tf_op jit(solution)/shard_map/ppermute | solution.py:169
  134.5 14.8 %all-to-all-start.3 = ((f32[16,16,128]{2,1,0:T(8,128)}), f32[16,16,128]{2,1,0:T(8,128)S(1)}, u32[]{:S(2)}, u32[]{:S(2)}) async-start(f32[16,16,128]{2,1,0:T(8,128)} %broadcast_in_dim.8), calls=%async_computation.3 | async-start | bytes 262144 | tf_op jit(solution)/shard_map/all_to_all | solution.py:163
  155.1 50.8 %all-to-all-start.1 = ((bf16[8,128,896]{2,1,0:T(8,128)(2,1)}), bf16[8,128,896]{2,1,0:T(8,128)(2,1)}, u32[]{:S(2)}, u32[]{:S(2)}) async-start(bf16[8,128,896]{2,1,0:T(8,128)(2,1)} %bitcast.79), calls=%async_computation.1 | async-start | bytes 3670016 | tf_op jit(solution)/shard_map/all_to_all | solution.py:171
  164.3 5.5 %collective-permute-start.14 = (f32[2,1024]{1,0:T(2,128)S(1)}, f32[2,1024]{1,0:T(2,128)S(1)}, u32[]{:S(2)}, u32[]{:S(2)}) collective-permute-start(f32[2,1024]{1,0:T(2,128)S(1)} %pad_maximum_fusion.1), channel_id=1, source_target_pairs={{0,1},{1,0},{2,3},{3,2},{4,5},{5,4},{6,7},{7,6},{8,9},{9,8},{10,11... | collective-permute-start | bytes 24584 | tf_op jit(solution)/shard_map/ppermute | solution.py:185
  169.9 7.0 %collective-permute-start.15 = (f32[2,1024]{1,0:T(2,128)S(1)}, f32[2,1024]{1,0:T(2,128)S(1)}, u32[]{:S(2)}, u32[]{:S(2)}) collective-permute-start(f32[2,1024]{1,0:T(2,128)S(1)} %fusion.35), channel_id=1, source_target_pairs={{0,2},{1,3},{2,0},{3,1},{4,6},{5,7},{6,4},{7,5},{8,10},{9,11},{10,... | collective-permute-start | bytes 24584 | tf_op jit(solution)/shard_map/ppermute | solution.py:185
  177.0 5.5 %collective-permute-start.16 = (f32[2,1024]{1,0:T(2,128)S(1)}, f32[2,1024]{1,0:T(2,128)S(1)}, u32[]{:S(2)}, u32[]{:S(2)}) collective-permute-start(f32[2,1024]{1,0:T(2,128)S(1)} %fusion.53), channel_id=1, source_target_pairs={{0,4},{1,5},{2,6},{3,7},{4,0},{5,1},{6,2},{7,3},{8,12},{9,13},{10,... | collective-permute-start | bytes 24584 | tf_op jit(solution)/shard_map/ppermute | solution.py:185
  182.5 6.4 %collective-permute-start.17 = (f32[2,1024]{1,0:T(2,128)S(1)}, f32[2,1024]{1,0:T(2,128)S(1)}, u32[]{:S(2)}, u32[]{:S(2)}) collective-permute-start(f32[2,1024]{1,0:T(2,128)S(1)} %add.104), channel_id=1, source_target_pairs={{0,8},{1,9},{2,10},{3,11},{4,12},{5,13},{6,14},{7,15},{8,0},{9,1},... | collective-permute-start | bytes 24584 | tf_op jit(solution)/shard_map/ppermute | solution.py:185
  188.9 9.4 %collective-permute-start.18 = (f32[2,1024]{1,0:T(2,128)S(1)}, f32[2,1024]{1,0:T(2,128)S(1)}, u32[]{:S(2)}, u32[]{:S(2)}) collective-permute-start(f32[2,1024]{1,0:T(2,128)S(1)} %add.105), channel_id=1, source_target_pairs={{0,16},{1,17},{2,18},{3,19},{4,20},{5,21},{6,22},{7,23},{8,24},{9,... | collective-permute-start | bytes 24584 | tf_op jit(solution)/shard_map/ppermute | solution.py:185
  (14 other events, 117.9 us)
